TPU v7x, 128 devices: a whole 4x4x4 slice. The times are simulated.
128 devices in a mesh: grp: 8 (over z, core), mem: 16 (over y, x).
Axes of the slice: x: 4, y: 4, z: 4, core: 2. Of those that a mesh axis runs over, the one named last changes fastest.
Arguments:
- forcing: float32 [3, 1024, 4096], P(None, ('grp', 'mem')), may hold values from -6 to 6
- viscosity: float32 [1024, 4096], P(('grp', 'mem')), may hold values from 0.1 to 10
- refinement: int32 [1024], P(('grp', 'mem')), may hold values from 0 to 1
- face_owner: int32 [4096, 1], P(('grp', 'mem')), may hold values from 0 to 15; in each aligned block of 32 rows (0 to 31, 32 to 63, ...) at most 4 rows name the same one
- face_block: int32 [1024, 4], P(('grp', 'mem')), may hold values from 0 to 7
- plane_block: int32 [1024, 2], P(('grp', 'mem')), may hold values from 0 to 7
- hanging: int32 [1024, 6], P(('grp', 'mem')), may hold values 0 or 1
- coarse_solver: float32 [8, 384, 384], P('grp', 'mem'), may hold values from -0.3125 to 0.3125
Outputs:
- velocity: float32 [3, 1024, 4096], P(None, ('grp', 'mem'))
- residual: float32 [3, 1024, 4096], P(None, ('grp', 'mem'))
Inputs may be any that keep to these rules, and one draw needn't show every extreme that they name: `face_owner`: among the 32 rows of one device no member appears more than 4 times, and some member appears exactly 4 times.
All inputs are finite; a program needn't handle non-finite values. No bound on the sum of `hanging` on one device may be relied on, other than what follows from the above.
Results may differ from a plain program's by a relative error of at most 0.0001.
Values sent between devices are 32-bit elements; how exact they have to be, the bound alone decides.
A program may use at most 64 MiB of HBM per device.

v0:
```python
import math
import jax
import jax.numpy as jnp
from jax import lax
from jax.sharding import PartitionSpec as P

EDGE = 16
DEG = 3
CELLS = 4096
FACE = 256
MASS_TERM = 1.0
LOWER_BOUND = 0.25
UPPER_BOUND = 2.0
HIGHEST = lax.Precision.HIGHEST


def shifted_2(block, axis, distance):
    devices = range(lax.axis_size(axis))
    route = [(i - distance, i) for i in devices if i - distance in devices]
    return lax.ppermute(block, axis, route)


def coarsen(plane_vals):
    leading = plane_vals.shape[:-1]
    squares = plane_vals.reshape(leading + (EDGE // 2, 2, EDGE // 2, 2))
    average = jnp.mean(squares, axis=(-3, -1), keepdims=True)
    return jnp.broadcast_to(average, squares.shape).reshape(leading + (FACE,))


def tables():
    lanes = jnp.arange(FACE, dtype=jnp.int32)
    lane_k = lanes % EDGE
    lane_j = lanes // EDGE
    sources = [lanes - 1, lanes + 1, lanes - EDGE, lanes + EDGE]
    valid = [lane_k > 0, lane_k < EDGE - 1, lane_j > 0, lane_j < EDGE - 1]
    shift_mat = jnp.concatenate(
        [
            ((lanes[:, None] == sources[d][None, :]) & valid[d][None, :]).astype(jnp.float32)
            for d in range(4)
        ],
        axis=1,
    )
    places = jnp.arange(EDGE, dtype=jnp.int32)
    picks = [places * EDGE, places * EDGE + EDGE - 1, places, (EDGE - 1) * EDGE + places]
    pick_mats = [(lanes[:, None] == picks[d][None, :]).astype(jnp.float32) for d in range(4)]
    return (shift_mat, pick_mats)


def far_faces(upper_planes, lower_planes, plane_block):
    arrived = []
    for by_step, outgoing in ((1, upper_planes), (-1, lower_planes)):
        arrived.append(shifted_2(outgoing, "grp", by_step))
    lower_ghost = jnp.take(arrived[0], plane_block[:, 0], axis=1)
    upper_ghost = jnp.take(arrived[1], plane_block[:, 1], axis=1)
    return (lower_ghost, upper_ghost)


def local(
    forcing, viscosity, refinement, face_owner, face_block, plane_block, hanging, coarse_solver
):
    blocks_here = forcing.shape[1]
    shift_mat, pick_mats = tables()
    pick_all = jnp.concatenate(pick_mats, axis=1)
    forcing_cube = forcing.reshape(3, blocks_here, EDGE, FACE)
    effective = (
        viscosity.reshape(blocks_here, EDGE, FACE)
        * jnp.exp2(-refinement.astype(jnp.float32))[:, None, None]
    )
    owners = face_owner[:, 0]
    opposite = jnp.array([1, 0, 3, 2], jnp.int32)
    wanted = (face_block * 4 + opposite[None, :]).reshape(-1)

    def near_faces(face_rows):
        gathered = lax.all_gather(face_rows, "mem", axis=0, tiled=True)
        return gathered[owners * (4 * blocks_here) + wanted]

    def ghost_set(stacked):
        channels = stacked.shape[0]
        picked = jnp.einsum("cbil,lm->cbim", stacked, pick_all, precision=HIGHEST)
        face_rows = (
            picked.reshape(channels, blocks_here, EDGE, 4, EDGE)
            .transpose(1, 3, 0, 2, 4)
            .reshape(blocks_here * 4, channels * FACE)
        )
        ghost_rows = near_faces(face_rows).reshape(blocks_here, 4, channels, FACE)
        result = [ghost_rows[:, direction].transpose(1, 0, 2) for direction in range(4)]
        lower_ghost, upper_ghost = far_faces(
            stacked[:, :, EDGE - 1, :], stacked[:, :, 0, :], plane_block
        )
        result.append(lower_ghost)
        result.append(upper_ghost)
        return [
            jnp.where(
                hanging[:, direction][None, :, None] == 1,
                coarsen(result[direction]),
                result[direction],
            )
            for direction in range(6)
        ]

    def beside(values, ghosts):
        channels = values.shape[0]
        shifted = jnp.einsum("cbil,lm->cbim", values, shift_mat, precision=HIGHEST)
        nearby = []
        for direction in range(4):
            placed = jnp.einsum(
                "cbim,lm->cbil",
                ghosts[direction].reshape(channels, blocks_here, EDGE, EDGE),
                pick_mats[direction],
                precision=HIGHEST,
            )
            nearby.append(shifted[..., direction * FACE : (direction + 1) * FACE] + placed)
        nearby.append(jnp.concatenate([ghosts[4][:, :, None, :], values[:, :, :-1, :]], axis=2))
        nearby.append(jnp.concatenate([values[:, :, 1:, :], ghosts[5][:, :, None, :]], axis=2))
        return nearby

    nearby_eff = beside(effective[None], ghost_set(effective[None]))
    weights = [0.5 * (effective + nearby_eff[direction][0]) for direction in range(6)]
    diagonal = MASS_TERM * effective
    for direction in range(6):
        diagonal = diagonal + weights[direction]

    def operate(values):
        nearby = beside(values, ghost_set(values))
        applied = diagonal * values
        for direction in range(6):
            applied = applied - weights[direction] * nearby[direction]
        return applied

    midpoint = 0.5 * (UPPER_BOUND + LOWER_BOUND)
    half_width = 0.5 * (UPPER_BOUND - LOWER_BOUND)
    sigma_ratio = midpoint / half_width

    def smooth(solution, residual):
        rho_now = 1.0 / sigma_ratio
        step_dir = residual / (diagonal * midpoint)
        for sweep_index in range(DEG):
            solution = solution + step_dir
            residual = residual - operate(step_dir)
            if sweep_index < DEG - 1:
                rho_next = 1.0 / (2.0 * sigma_ratio - rho_now)
                step_dir = rho_next * rho_now * step_dir + 2.0 * rho_next / half_width * (
                    residual / diagonal
                )
                rho_now = rho_next
        return (solution, residual)

    solution, residual = smooth(jnp.zeros_like(forcing_cube), forcing_cube)
    coarse_local = (jnp.sum(residual, axis=(2, 3)) / math.sqrt(CELLS)).T.reshape(-1)
    rows_here = coarse_solver[0]
    correction = jnp.dot(
        rows_here,
        lax.all_gather(coarse_local, "mem", axis=0, tiled=True),
        precision=HIGHEST,
        preferred_element_type=jnp.float32,
    )
    lifted = jnp.broadcast_to(
        correction.reshape(blocks_here, 3).T[:, :, None, None], forcing_cube.shape
    )
    solution = solution + lifted
    residual = residual - operate(lifted)
    solution, residual = smooth(solution, residual)
    return (solution.reshape(forcing.shape), residual.reshape(forcing.shape))


def solution(mesh):
    in_specs = (
        P(None, ("grp", "mem"), None),
        P(("grp", "mem"), None),
        P(("grp", "mem")),
        P(("grp", "mem"), None),
        P(("grp", "mem"), None),
        P(("grp", "mem"), None),
        P(("grp", "mem"), None),
        P("grp", "mem", None),
    )
    out_specs = (P(None, ("grp", "mem"), None), P(None, ("grp", "mem"), None))
    return jax.shard_map(local, mesh=mesh, in_specs=in_specs, out_specs=out_specs, check_vma=False)
```

profile of v0, /device:TPU:0, one launch (start us, length us, event | category | flops | bytes accessed | tf_op | source)
XLA Modules:
  0.0 607.3 jit_solution(15840290535157774675)
XLA Ops:
  14.4 24.8 %all_gather.27 = f32[512,256]{1,0:T(8,128)S(1)} all-gather(f32[32,256]{1,0:T(8,128)S(1)} %reshape.1007), channel_id=1, replica_groups=mesh['grp'=8,'mem'=16] {'mem'}, dimensions={0}, use_global_device_ids=true | all-gather | bytes 557056 | tf_op jit(solution)/shard_map/all_gather | solution.py:74
  71.7 24.8 %all-gather.8.cloned.1.call-done = f32[512,768]{1,0:T(8,128)} async-done(((f32[32,768]{1,0:T(8,128)}), f32[512,768]{1,0:T(8,128)}) %all-gather.8.cloned.1.call-update) | async-done | bytes 1572880 | tf_op jit(solution)/shard_map/all_gather | solution.py:74
  96.5 2.2 gather_fusion.1
  129.4 2.1 gather_fusion.12
  134.5 2.0 reduce_sum.457
  138.3 1.7 copy.571
  142.9 2.0 gather_fusion.13
  148.0 1.9 reduce_sum.458
  151.7 1.7 copy.576
  154.9 11.5 %all-gather.10.cloned.1.call-done = f32[512,768]{1,0:T(8,128)} async-done(((f32[32,768]{1,0:T(8,128)}), f32[512,768]{1,0:T(8,128)}) %all-gather.10.cloned.1.call-update) | async-done | bytes 1572880 | tf_op jit(solution)/shard_map/all_gather | solution.py:74
  166.4 2.8 gather_fusion.2
  172.3 1.7 copy.553
  174.0 2.0 reduce_sum.453
  177.7 1.8 copy.554
  179.5 1.7 copy.557
  181.1 2.0 reduce_sum.454
  184.9 1.8 copy.558
  186.6 1.7 copy.561
  188.3 2.0 reduce_sum.455
  192.0 1.8 copy.562
  193.8 1.7 copy.565
  195.5 1.9 reduce_sum.456
  199.2 1.8 copy.566
  226.1 2.0 fusion.97
  229.0 1.7 collective-permute-start.7
  236.2 28.4 %all-gather.12.cloned.1.call-done = f32[512,768]{1,0:T(8,128)} async-done(((f32[32,768]{1,0:T(8,128)}), f32[512,768]{1,0:T(8,128)}) %all-gather.12.cloned.1.call-update) | async-done | bytes 1572880 | tf_op jit(solution)/shard_map/all_gather | solution.py:74
  264.5 2.2 gather_fusion.3
  281.1 38.1 %all-reduce = f32[384]{0:T(512)S(1)} all-reduce(f32[384]{0:T(512)S(1)} %dynamic-update-slice), channel_id=1, replica_groups=mesh['grp'=8,'mem'=16] {'mem'}, use_global_device_ids=true, to_apply=%add | all-reduce | flops 384 | bytes 3072
  321.0 2.1 reshape.1069
  324.6 2.0 fusion.95
  333.9 29.4 %all-gather.14.cloned.1.call-done = f32[512,768]{1,0:T(8,128)} async-done(((f32[32,768]{1,0:T(8,128)}), f32[512,768]{1,0:T(8,128)}) %all-gather.14.cloned.1.call-update) | async-done | bytes 1572880 | tf_op jit(solution)/shard_map/all_gather | solution.py:74
  363.2 2.2 gather_fusion.4
  380.8 2.0 fusion.93
  401.3 21.2 %all-gather.16.cloned.1.call-done = f32[512,768]{1,0:T(8,128)} async-done(((f32[32,768]{1,0:T(8,128)}), f32[512,768]{1,0:T(8,128)}) %all-gather.16.cloned.1.call-update) | async-done | bytes 1572880 | tf_op jit(solution)/shard_map/all_gather | solution.py:74
  422.5 2.2 gather_fusion.5
  450.0 2.1 copy.658
  452.1 2.1 reshape.1107
  455.6 2.0 fusion.91
  476.4 21.0 %all-gather.18.cloned.1.call-done = f32[512,768]{1,0:T(8,128)} async-done(((f32[32,768]{1,0:T(8,128)}), f32[512,768]{1,0:T(8,128)}) %all-gather.18.cloned.1.call-update) | async-done | bytes 1572880 | tf_op jit(solution)/shard_map/all_gather | solution.py:74
  497.3 2.2 gather_fusion.6
  526.1 1.9 collective-permute-start.14
  531.8 1.8 reshape.1125
  546.6 22.0 %all-gather.20.cloned.1.call-done = f32[512,768]{1,0:T(8,128)} async-done(((f32[32,768]{1,0:T(8,128)}), f32[512,768]{1,0:T(8,128)}) %all-gather.20.cloned.1.call-update) | async-done | bytes 1572880 | tf_op jit(solution)/shard_map/all_gather | solution.py:74
  568.5 2.2 gather_fusion.7
  575.7 1.7 copy.691
  579.6 1.8 copy.692
  585.3 1.8 copy.696
  590.9 1.8 copy.700
  (852 shorter events, 291.5 us)
Async XLA Ops:
  7.2 32.1 %copy-start.144 = (s32[4]{0:T(128)S(1)}, s32[4]{0:T(128)}, u32[]{:S(2)}) copy-start(s32[4]{0:T(128)} %constant.145.clone) | copy-start | bytes 52
  7.2 32.1 %copy-start.142 = (s32[8,4]{0,1:T(4,128)S(1)}, s32[8,4]{0,1:T(4,128)}, u32[]{:S(2)}) copy-start(s32[8,4]{0,1:T(4,128)} %param.17) | copy-start | bytes 388
  7.2 32.3 %copy-start.145 = (s32[32,1]{0,1:T(1,128)S(1)}, s32[32,1]{0,1:T(1,128)}, u32[]{:S(2)}) copy-start(s32[32,1]{0,1:T(1,128)} %param.16) | copy-start | bytes 388
  7.2 89.3 %all-gather.8.cloned.1.call-start = ((), (), s32[]{:S(2)}) async-start(), calls=%async_computation | async-start | bytes 1671168 | tf_op jit(solution)/shard_map/all_gather | solution.py:74
  7.9 39.2 %copy-start.140 = (f32[8]{0:T(128)}, f32[8]{0:T(128)S(1)}, u32[]{:S(2)}) copy-start(f32[8]{0:T(128)S(1)} %multiply_exponential_fusion) | copy-start | bytes 100
  8.9 35.8 %collective-permute-start = (f32[1,8,256]{2,0,1:T(1,128)S(1)}, f32[1,8,256]{2,0,1:T(1,128)S(1)}, u32[]{:S(2)}, u32[]{:S(2)}) collective-permute-start(f32[1,8,256]{2,0,1:T(1,128)S(1)} %get-tuple-element.104), channel_id=1, source_target_pairs={{0,16},{16,32},{32,48},{48,64},{64,80},{80,96},{96,112},{1,17},{17... | collective-permute-start | bytes 24584 | tf_op jit(solution)/shard_map/ppermute | solution.py:20
  10.2 35.6 %collective-permute-start.1 = (f32[1,8,256]{2,0,1:T(1,128)S(1)}, f32[1,8,256]{2,0,1:T(1,128)S(1)}, u32[]{:S(2)}, u32[]{:S(2)}) collective-permute-start(f32[1,8,256]{2,0,1:T(1,128)S(1)} %get-tuple-element.105), channel_id=1, source_target_pairs={{16,0},{32,16},{48,32},{64,48},{80,64},{96,80},{112,96},{17,1},{33... | collective-permute-start | bytes 24584 | tf_op jit(solution)/shard_map/ppermute | solution.py:20
  11.5 32.2 %copy-start.129 = (s32[16]{0:T(128)}, s32[16]{0:T(128)S(1)}, u32[]{:S(2)}) copy-start(s32[16]{0:T(128)S(1)} %iota_add_fusion.4) | copy-start | bytes 196
  11.5 31.4 %copy-start.122 = (s32[16]{0:T(128)}, s32[16]{0:T(128)S(1)}, u32[]{:S(2)}) copy-start(s32[16]{0:T(128)S(1)} %broadcast_add_fusion) | copy-start | bytes 196
  11.6 31.1 %copy-start.127 = (s32[16]{0:T(128)}, s32[16]{0:T(128)S(1)}, u32[]{:S(2)}) copy-start(s32[16]{0:T(128)S(1)} %iota_multiply_fusion) | copy-start | bytes 196
  11.6 29.4 %copy-start.70 = (s32[8,6]{1,0:T(8,128)S(1)}, s32[8,6]{1,0:T(8,128)}, u32[]{:S(2)}) copy-start(s32[8,6]{1,0:T(8,128)} %param.19) | copy-start | bytes 580
  41.4 5.6 copy-start.118
  49.7 116.8 %all-gather.10.cloned.1.call-start = ((), (), s32[]{:S(2)}) async-start(), calls=%async_computation.1 | async-start | bytes 1671168 | tf_op jit(solution)/shard_map/all_gather | solution.py:74
  49.9 5.5 collective-permute-start.2
  51.9 11.4 %collective-permute-start.3 = (f32[3,8,256]{2,1,0:T(8,128)}, f32[3,8,256]{2,1,0:T(8,128)}, u32[]{:S(2)}, u32[]{:S(2)}) collective-permute-start(f32[3,8,256]{2,1,0:T(8,128)} %bitcast.760), channel_id=1, source_target_pairs={{16,0},{32,16},{48,32},{64,48},{80,64},{96,80},{112,96},{17,1},{33... | collective-permute-start | bytes 73736 | tf_op jit(solution)/shard_map/ppermute | solution.py:20
  123.3 141.2 %all-gather.12.cloned.1.call-start = ((), (), s32[]{:S(2)}) async-start(), calls=%async_computation.2 | async-start | bytes 1671168 | tf_op jit(solution)/shard_map/all_gather | solution.py:74
  123.4 5.3 collective-permute-start.4
  125.6 89.6 %copy-start.1 = (f32[3,8,16,1024]{3,2,1,0:T(8,128)}, f32[3,8,16,1024]{3,2,1,0:T(8,128)S(1)}, u32[]{:S(2)}) copy-start(f32[3,8,16,1024]{3,2,1,0:T(8,128)S(1)} %fusion.99) | copy-start | bytes 4718596
  127.2 14.3 %collective-permute-start.5 = (f32[3,8,256]{2,1,0:T(8,128)}, f32[3,8,256]{2,1,0:T(8,128)}, u32[]{:S(2)}, u32[]{:S(2)}) collective-permute-start(f32[3,8,256]{2,1,0:T(8,128)} %bitcast.758), channel_id=1, source_target_pairs={{16,0},{32,16},{48,32},{64,48},{80,64},{96,80},{112,96},{17,1},{33... | collective-permute-start | bytes 73736 | tf_op jit(solution)/shard_map/ppermute | solution.py:20
  221.4 141.8 %all-gather.14.cloned.1.call-start = ((), (), s32[]{:S(2)}) async-start(), calls=%async_computation.3 | async-start | bytes 1671168 | tf_op jit(solution)/shard_map/all_gather | solution.py:74
  224.8 6.7 %copy-start.72 = (pred[8]{0:T(512)(128)(4,1)S(1)}, pred[8]{0:T(512)(128)(4,1)}, u32[]{:S(2)}) copy-start(pred[8]{0:T(512)(128)(4,1)} %copy-done.71) | copy-start | bytes 28
  224.8 6.0 collective-permute-start.6
  229.0 5.6 copy-start.78
  229.0 4.9 collective-permute-start.7
  279.4 39.8 %copy-start.69 = (f32[8,3,384]{2,1,0:T(4,128)S(1)}, f32[8,3,384]{2,1,0:T(4,128)}, u32[]{:S(2)}) copy-start(f32[8,3,384]{2,1,0:T(4,128)} %dot_general.197) | copy-start | bytes 110596
  319.5 51.4 %copy-start.99 = (f32[1,8,3]{1,2,0:T(4,128)}, f32[1,8,3]{1,2,0:T(4,128)S(1)}, u32[]{:S(2)}) copy-start(f32[1,8,3]{1,2,0:T(4,128)S(1)} %copy.721) | copy-start | bytes 292
  321.0 7.9 %copy-start.73 = (pred[8]{0:T(512)(128)(4,1)S(1)}, pred[8]{0:T(512)(128)(4,1)}, u32[]{:S(2)}) copy-start(pred[8]{0:T(512)(128)(4,1)} %copy-done.71) | copy-start | bytes 28
  323.1 99.3 %all-gather.16.cloned.1.call-start = ((), (), s32[]{:S(2)}) async-start(), calls=%async_computation.4 | async-start | bytes 1671168 | tf_op jit(solution)/shard_map/all_gather | solution.py:74
  323.3 4.9 collective-permute-start.8
  326.6 5.7 copy-start.79
  326.6 5.0 collective-permute-start.9
  379.4 118.0 %all-gather.18.cloned.1.call-start = ((), (), s32[]{:S(2)}) async-start(), calls=%async_computation.5 | async-start | bytes 1671168 | tf_op jit(solution)/shard_map/all_gather | solution.py:74
  379.5 7.5 %copy-start.74 = (pred[8]{0:T(512)(128)(4,1)S(1)}, pred[8]{0:T(512)(128)(4,1)}, u32[]{:S(2)}) copy-start(pred[8]{0:T(512)(128)(4,1)} %copy-done.71) | copy-start | bytes 28
  379.5 6.2 %collective-permute-start.10 = (f32[3,8,256]{2,1,0:T(8,128)S(1)}, f32[3,8,256]{2,1,0:T(8,128)S(1)}, u32[]{:S(2)}, u32[]{:S(2)}) collective-permute-start(f32[3,8,256]{2,1,0:T(8,128)S(1)} %bitcast.936), channel_id=1, source_target_pairs={{0,16},{16,32},{32,48},{48,64},{64,80},{80,96},{96,112},{1,17},{17... | collective-permute-start | bytes 73736 | tf_op jit(solution)/shard_map/ppermute | solution.py:20
  384.2 8.6 %collective-permute-start.11 = (f32[3,8,256]{2,1,0:T(8,128)}, f32[3,8,256]{2,1,0:T(8,128)}, u32[]{:S(2)}, u32[]{:S(2)}) collective-permute-start(f32[3,8,256]{2,1,0:T(8,128)} %bitcast.754), channel_id=1, source_target_pairs={{16,0},{32,16},{48,32},{64,48},{80,64},{96,80},{112,96},{17,1},{33... | collective-permute-start | bytes 73736 | tf_op jit(solution)/shard_map/ppermute | solution.py:20
  454.2 114.3 %all-gather.20.cloned.1.call-start = ((), (), s32[]{:S(2)}) async-start(), calls=%async_computation.6 | async-start | bytes 1671168 | tf_op jit(solution)/shard_map/all_gather | solution.py:74
  454.3 7.7 %copy-start.75 = (pred[8]{0:T(512)(128)(4,1)S(1)}, pred[8]{0:T(512)(128)(4,1)}, u32[]{:S(2)}) copy-start(pred[8]{0:T(512)(128)(4,1)} %copy-done.71) | copy-start | bytes 28
  454.3 6.4 %collective-permute-start.12 = (f32[3,8,256]{2,1,0:T(8,128)S(1)}, f32[3,8,256]{2,1,0:T(8,128)S(1)}, u32[]{:S(2)}, u32[]{:S(2)}) collective-permute-start(f32[3,8,256]{2,1,0:T(8,128)S(1)} %bitcast.937), channel_id=1, source_target_pairs={{0,16},{16,32},{32,48},{48,64},{64,80},{80,96},{96,112},{1,17},{17... | collective-permute-start | bytes 73736 | tf_op jit(solution)/shard_map/ppermute | solution.py:20
  459.2 8.7 %collective-permute-start.13 = (f32[3,8,256]{2,1,0:T(8,128)}, f32[3,8,256]{2,1,0:T(8,128)}, u32[]{:S(2)}, u32[]{:S(2)}) collective-permute-start(f32[3,8,256]{2,1,0:T(8,128)} %bitcast.752), channel_id=1, source_target_pairs={{16,0},{32,16},{48,32},{64,48},{80,64},{96,80},{112,96},{17,1},{33... | collective-permute-start | bytes 73736 | tf_op jit(solution)/shard_map/ppermute | solution.py:20
  526.1 7.5 %collective-permute-start.14 = (f32[3,8,256]{2,1,0:T(8,128)}, f32[3,8,256]{2,1,0:T(8,128)}, u32[]{:S(2)}, u32[]{:S(2)}) collective-permute-start(f32[3,8,256]{2,1,0:T(8,128)} %bitcast.751), channel_id=1, source_target_pairs={{0,16},{16,32},{32,48},{48,64},{64,80},{80,96},{96,112},{1,17},{17... | collective-permute-start | bytes 73736 | tf_op jit(solution)/shard_map/ppermute | solution.py:20
  528.5 6.5 %collective-permute-start.15 = (f32[3,8,256]{2,1,0:T(8,128)}, f32[3,8,256]{2,1,0:T(8,128)}, u32[]{:S(2)}, u32[]{:S(2)}) collective-permute-start(f32[3,8,256]{2,1,0:T(8,128)} %bitcast.750), channel_id=1, source_target_pairs={{16,0},{32,16},{48,32},{64,48},{80,64},{96,80},{112,96},{17,1},{33... | collective-permute-start | bytes 73736 | tf_op jit(solution)/shard_map/ppermute | solution.py:20
  530.9 5.6 copy-start.76
  531.8 9.1 %copy-start.121 = (pred[8]{0:T(512)(128)(4,1)S(1)}, pred[8]{0:T(512)(128)(4,1)}, u32[]{:S(2)}) copy-start(pred[8]{0:T(512)(128)(4,1)} %copy-done.118) | copy-start | bytes 28
  538.9 7.0 %copy-start.117 = (pred[8]{0:T(512)(128)(4,1)S(1)}, pred[8]{0:T(512)(128)(4,1)}, u32[]{:S(2)}) copy-start(pred[8]{0:T(512)(128)(4,1)} %copy-done.114) | copy-start | bytes 28
  584.4 8.3 %copy-start.104 = (pred[8]{0:T(512)(128)(4,1)S(1)}, pred[8]{0:T(512)(128)(4,1)}, u32[]{:S(2)}) copy-start(pred[8]{0:T(512)(128)(4,1)} %copy-done.102) | copy-start | bytes 28
  584.4 8.3 %copy-start.107 = (pred[8]{0:T(512)(128)(4,1)S(1)}, pred[8]{0:T(512)(128)(4,1)}, u32[]{:S(2)}) copy-start(pred[8]{0:T(512)(128)(4,1)} %copy-done.105) | copy-start | bytes 28
  584.4 8.3 %copy-start.110 = (pred[8]{0:T(512)(128)(4,1)S(1)}, pred[8]{0:T(512)(128)(4,1)}, u32[]{:S(2)}) copy-start(pred[8]{0:T(512)(128)(4,1)} %copy-done.108) | copy-start | bytes 28
  584.4 8.3 %copy-start.113 = (pred[8]{0:T(512)(128)(4,1)S(1)}, pred[8]{0:T(512)(128)(4,1)}, u32[]{:S(2)}) copy-start(pred[8]{0:T(512)(128)(4,1)} %copy-done.111) | copy-start | bytes 28
  (121 other events, 217.3 us)
Sparse Core Ops, SparseCore 0:
  49.8 46.6 all-gather.7
  123.5 42.9 all-gather.9
  221.5 42.9 all-gather.11
  323.3 39.9 all-gather.13
  379.5 42.9 all-gather.15
  454.3 42.9 all-gather.17
  525.5 42.9 all-gather.19
where the time goes:
time: 620 us; the launch traced here: 607 us
  local copies, waits for them, and re-layouts  207 us (33%)
  waiting for transfers between devices  160 us (26%)
  other arithmetic  92.3 us (15%)
  blocking collectives  62.9 us (10%)
  matrix products  41.7 us (7%)
  starting transfers between devices  23.6 us (4%)
  between operations  19.2 us (3%)
    all_gather x7, waiting for transfers between devices, near_faces(): gathered = lax.all_gather(face_rows, 'mem', axis=0, tiled=True)  158 us
    reduce_sum x48, other arithmetic, coarsen(): average = jnp.mean(squares, axis=(-3, -1), keepdims=True)  42 us
    unnamed x1, blocking collectives  38.1 us
    reshape x42, local copies, waits for them, and re-layouts, coarsen(): return jnp.broadcast_to(average, squares.shape).reshape(leading + (FACE,))  35.4 us
    transpose x35, local copies, waits for them, and re-layouts, ghost_set(): ghost_rows[:, direction].transpose(1, 0, 2)  31.4 us
    dot_general x32, matrix products, beside(): jnp.einsum('cbim,lm->cbil', ghosts[direction].reshape(channels, blocks_he...  27.8 us
    all_gather x1, blocking collectives, near_faces(): gathered = lax.all_gather(face_rows, 'mem', axis=0, tiled=True)  24.8 us
    ppermute x16, starting transfers between devices, shifted_2(): return lax.ppermute(block, axis, route)  23.3 us
  transfers between devices with their start and end apart: 23, of which 9 were waited for; matrix products, arithmetic and copies ran while one was open for 20% of the time, Pallas kernels for 0%

commit v1 on v0

--- a/solution.py
+++ b/solution.py
@@ -1,3 +1,4 @@
+import functools
 import math
 import jax
 import jax.numpy as jnp
@@ -12,6 +13,32 @@
 LOWER_BOUND = 0.25
 UPPER_BOUND = 2.0
 HIGHEST = lax.Precision.HIGHEST
+
+
+def watch_stacks_all(arr, dimension_no):
+    base_arr, later, e_next = (lax.axis_size("mem"), lax.axis_index("mem"), arr.shape[dimension_no])
+    in_order = tuple(((i0, (i0 + 1) % base_arr) for i0 in range(base_arr)))
+    table = tuple(((i0, (i0 - 1) % base_arr) for i0 in range(base_arr)))
+    tall = jnp.zeros(
+        (*arr.shape[:dimension_no], base_arr * e_next, *arr.shape[dimension_no + 1 :]), arr.dtype
+    )
+    tall = lax.dynamic_update_slice_in_dim(tall, arr, later * e_next, axis=dimension_no)
+    part_next = block_last = arr
+    parts_out = base_arr // 2
+    for ix in tuple(range(1, parts_out + 1)):
+        part_next = lax.ppermute(part_next, "mem", in_order)
+        tall = lax.dynamic_update_slice_in_dim(
+            tall, part_next, (later - ix) % base_arr * e_next, axis=dimension_no
+        )
+        if ix < base_arr - parts_out:
+            block_last = lax.ppermute(block_last, "mem", table)
+            tall = lax.dynamic_update_slice_in_dim(
+                tall, block_last, (later + ix) % base_arr * e_next, axis=dimension_no
+            )
+    return tall
+
+
+panel_edit = functools.partial(watch_stacks_all, dimension_no=0)
 
 
 def shifted_2(block, axis, distance):
@@ -71,7 +98,7 @@
     wanted = (face_block * 4 + opposite[None, :]).reshape(-1)
 
     def near_faces(face_rows):
-        gathered = lax.all_gather(face_rows, "mem", axis=0, tiled=True)
+        gathered = panel_edit(face_rows)
         return gathered[owners * (4 * blocks_here) + wanted]
 
     def ghost_set(stacked):

time: 620 us -> 943 us (1.52)
  the two profiles are of different devices: /device:TPU:0 before, /device:TPU:96 now
where the time goes in v1:
time: 943 us; the launch traced here: 927 us
  starting transfers between devices  357 us (38%)
  local copies, waits for them, and re-layouts  288 us (31%)
  waiting for transfers between devices  108 us (11%)
  other arithmetic  91.3 us (10%)
  matrix products  41.3 us (4%)
  blocking collectives  35.4 us (4%)
    ppermute x56, starting transfers between devices, watch_stacks_all(): block_last = lax.ppermute(block_last, 'mem', table)  308 us
    ppermute x64, waiting for transfers between devices, watch_stacks_all(): part_next = lax.ppermute(part_next, 'mem', in_order)  98 us
    ppermute x16, starting transfers between devices, shifted_2(): return lax.ppermute(block, axis, route)  43.7 us
    dynamic_update_slice x64, local copies, waits for them, and re-layouts, watch_stacks_all(): lax.dynamic_update_slice_in_dim(tall, part_next, (later - ix) % base_arr...  41.6 us
    dynamic_update_slice x56, local copies, waits for them, and re-layouts, watch_stacks_all(): lax.dynamic_update_slice_in_dim(tall, block_last, (later + ix) % base_arr...  35.9 us
    reduce_sum x48, other arithmetic, coarsen(): average = jnp.mean(squares, axis=(-3, -1), keepdims=True)  35.8 us
    unnamed x1, blocking collectives  35.4 us
    reshape x42, local copies, waits for them, and re-layouts, coarsen(): return jnp.broadcast_to(average, squares.shape).reshape(leading + (FACE,))  28.8 us
  transfers between devices with their start and end apart: 136, of which 76 were waited for; matrix products, arithmetic and copies ran while one was open for 22% of the time, Pallas kernels for 0%

profile of v1, /device:TPU:96, one launch (start us, length us, event | category | flops | bytes accessed | tf_op | source)
XLA Modules:
  0.0 926.7 jit_solution(15187204219219680091)
XLA Ops:
  50.3 5.5 collective-permute-start.11
  57.5 5.5 collective-permute-start.13
  64.8 7.2 collective-permute-done.14
  77.9 5.8 collective-permute-start.18
  122.0 5.6 collective-permute-start.22
  129.9 5.7 collective-permute-start.24
  137.8 5.7 collective-permute-start.26
  145.7 5.7 collective-permute-start.28
  154.4 5.8 collective-permute-start.30
  163.1 6.6 collective-permute-done.31
  248.1 5.4 collective-permute-start.37
  255.9 5.6 collective-permute-start.39
  263.8 5.7 collective-permute-start.41
  271.7 6.0 collective-permute-start.43
  279.9 5.7 collective-permute-start.45
  288.5 5.8 collective-permute-start.47
  297.1 6.5 collective-permute-done.48
  384.3 5.4 collective-permute-start.54
  392.0 5.6 collective-permute-start.56
  399.9 5.6 collective-permute-start.58
  407.8 5.6 collective-permute-start.60
  415.8 5.6 collective-permute-start.62
  424.3 5.8 collective-permute-start.64
  433.2 6.6 collective-permute-done.65
  457.1 35.4 %all-reduce = f32[384]{0:T(512)S(1)} all-reduce(f32[384]{0:T(512)S(1)} %dynamic-update-slice), channel_id=1, replica_groups=mesh['grp'=8,'mem'=16] {'mem'}, use_global_device_ids=true, to_apply=%add | all-reduce | flops 384 | bytes 3072
  540.0 5.4 collective-permute-start.77
  548.0 5.5 collective-permute-start.79
  566.1 6.6 collective-permute-done.82
  624.2 5.4 collective-permute-start.88
  632.1 5.6 collective-permute-start.90
  639.9 5.7 collective-permute-start.92
  647.9 6.1 collective-permute-start.94
  656.2 5.7 collective-permute-start.96
  664.8 5.8 collective-permute-start.98
  673.4 6.4 collective-permute-done.99
  747.8 5.4 collective-permute-start.105
  755.7 5.6 collective-permute-start.107
  763.5 5.7 collective-permute-start.109
  771.4 5.7 collective-permute-start.111
  779.4 5.7 collective-permute-start.113
  787.8 5.8 collective-permute-start.115
  796.9 6.6 collective-permute-done.116
  862.1 5.6 collective-permute-start.124
  869.9 5.7 collective-permute-start.126
  877.8 5.7 collective-permute-start.128
  885.8 5.7 collective-permute-start.130
  894.4 5.8 collective-permute-start.132
  903.1 6.6 collective-permute-done.133
  (1196 shorter events, 611.0 us)
Async XLA Ops:
  3.2 18.1 %collective-permute-start = (f32[32,256]{1,0:T(8,128)S(1)}, f32[32,256]{1,0:T(8,128)S(1)}, u32[]{:S(2)}, u32[]{:S(2)}) collective-permute-start(f32[32,256]{1,0:T(8,128)S(1)} %reshape.1007), channel_id=1, source_target_pairs={{0,1},{1,2},{2,3},{3,4},{4,5},{5,6},{6,7},{7,8},{8,9},{9,10},{10,1... | collective-permute-start | bytes 98312 | tf_op jit(solution)/shard_map/ppermute | solution.py:29
  4.7 16.6 %collective-permute-start.1 = (f32[32,256]{1,0:T(8,128)S(1)}, f32[32,256]{1,0:T(8,128)S(1)}, u32[]{:S(2)}, u32[]{:S(2)}) collective-permute-start(f32[32,256]{1,0:T(8,128)S(1)} %reshape.1007), channel_id=1, source_target_pairs={{0,15},{1,0},{2,1},{3,2},{4,3},{5,4},{6,5},{7,6},{8,7},{9,8},{10,9... | collective-permute-start | bytes 98312 | tf_op jit(solution)/shard_map/ppermute | solution.py:34
  9.6 9.3 %collective-permute-start.15 = (f32[1,8,256]{2,0,1:T(1,128)S(1)}, f32[1,8,256]{2,0,1:T(1,128)S(1)}, u32[]{:S(2)}, u32[]{:S(2)}) collective-permute-start(f32[1,8,256]{2,0,1:T(1,128)S(1)} %get-tuple-element.104), channel_id=1, source_target_pairs={{0,16},{16,32},{32,48},{48,64},{64,80},{80,96},{96,112},{1,17},{17... | collective-permute-start | bytes 24584 | tf_op jit(solution)/shard_map/ppermute | solution.py:47
  77.9 34.7 %collective-permute-start.17 = (f32[32,768]{1,0:T(8,128)}, f32[32,768]{1,0:T(8,128)}, u32[]{:S(2)}, u32[]{:S(2)}) collective-permute-start(f32[32,768]{1,0:T(8,128)} %reshape.1012), channel_id=1, source_target_pairs={{0,1},{1,2},{2,3},{3,4},{4,5},{5,6},{6,7},{7,8},{8,9},{9,10},{10,1... | collective-permute-start | bytes 294920 | tf_op jit(solution)/shard_map/ppermute | solution.py:29
  77.9 36.2 %collective-permute-start.18 = (f32[32,768]{1,0:T(8,128)}, f32[32,768]{1,0:T(8,128)}, u32[]{:S(2)}, u32[]{:S(2)}) collective-permute-start(f32[32,768]{1,0:T(8,128)} %reshape.1012), channel_id=1, source_target_pairs={{0,15},{1,0},{2,1},{3,2},{4,3},{5,4},{6,5},{7,6},{8,7},{9,8},{10,9... | collective-permute-start | bytes 294920 | tf_op jit(solution)/shard_map/ppermute | solution.py:34
  86.6 8.9 collective-permute-start.32
  91.9 10.8 %collective-permute-start.33 = (f32[3,8,256]{2,1,0:T(8,128)}, f32[3,8,256]{2,1,0:T(8,128)}, u32[]{:S(2)}, u32[]{:S(2)}) collective-permute-start(f32[3,8,256]{2,1,0:T(8,128)} %bitcast.764), channel_id=1, source_target_pairs={{16,0},{32,16},{48,32},{64,48},{80,64},{96,80},{112,96},{17,1},{33... | collective-permute-start | bytes 73736 | tf_op jit(solution)/shard_map/ppermute | solution.py:47
  112.6 8.5 collective-permute-start.19
  145.7 8.6 collective-permute-start.28
  152.8 8.8 collective-permute-start.29
  202.6 43.9 %collective-permute-start.34 = (f32[32,768]{1,0:T(8,128)}, f32[32,768]{1,0:T(8,128)}, u32[]{:S(2)}, u32[]{:S(2)}) collective-permute-start(f32[32,768]{1,0:T(8,128)} %reshape.1031), channel_id=1, source_target_pairs={{0,1},{1,2},{2,3},{3,4},{4,5},{5,6},{6,7},{7,8},{8,9},{9,10},{10,1... | collective-permute-start | bytes 294920 | tf_op jit(solution)/shard_map/ppermute | solution.py:29
  202.6 45.4 %collective-permute-start.35 = (f32[32,768]{1,0:T(8,128)}, f32[32,768]{1,0:T(8,128)}, u32[]{:S(2)}, u32[]{:S(2)}) collective-permute-start(f32[32,768]{1,0:T(8,128)} %reshape.1031), channel_id=1, source_target_pairs={{0,15},{1,0},{2,1},{3,2},{4,3},{5,4},{6,5},{7,6},{8,7},{9,8},{10,9... | collective-permute-start | bytes 294920 | tf_op jit(solution)/shard_map/ppermute | solution.py:34
  209.9 9.0 collective-permute-start.49
  215.2 16.4 %collective-permute-start.50 = (f32[3,8,256]{2,1,0:T(8,128)}, f32[3,8,256]{2,1,0:T(8,128)}, u32[]{:S(2)}, u32[]{:S(2)}) collective-permute-start(f32[3,8,256]{2,1,0:T(8,128)} %bitcast.762), channel_id=1, source_target_pairs={{16,0},{32,16},{48,32},{64,48},{80,64},{96,80},{112,96},{17,1},{33... | collective-permute-start | bytes 73736 | tf_op jit(solution)/shard_map/ppermute | solution.py:47
  246.5 8.5 collective-permute-start.36
  279.9 8.6 collective-permute-start.45
  286.7 9.0 collective-permute-start.46
  359.2 23.5 %collective-permute-start.51 = (f32[32,768]{1,0:T(8,128)}, f32[32,768]{1,0:T(8,128)}, u32[]{:S(2)}, u32[]{:S(2)}) collective-permute-start(f32[32,768]{1,0:T(8,128)} %reshape.1050), channel_id=1, source_target_pairs={{0,1},{1,2},{2,3},{3,4},{4,5},{5,6},{6,7},{7,8},{8,9},{9,10},{10,1... | collective-permute-start | bytes 294920 | tf_op jit(solution)/shard_map/ppermute | solution.py:29
  359.2 25.1 %collective-permute-start.52 = (f32[32,768]{1,0:T(8,128)}, f32[32,768]{1,0:T(8,128)S(1)}, u32[]{:S(2)}, u32[]{:S(2)}) collective-permute-start(f32[32,768]{1,0:T(8,128)} %reshape.1050), channel_id=1, source_target_pairs={{0,15},{1,0},{2,1},{3,2},{4,3},{5,4},{6,5},{7,6},{8,7},{9,8},{10,9... | collective-permute-start | bytes 294920 | tf_op jit(solution)/shard_map/ppermute | solution.py:34
  390.8 8.4 collective-permute-start.55
  415.1 8.4 collective-permute-start.61
  415.8 8.5 collective-permute-start.62
  423.5 8.4 collective-permute-start.63
  495.7 19.8 %collective-permute-start.68 = (f32[32,768]{1,0:T(8,128)S(1)}, f32[32,768]{1,0:T(8,128)S(1)}, u32[]{:S(2)}, u32[]{:S(2)}) collective-permute-start(f32[32,768]{1,0:T(8,128)S(1)} %reshape.1069), channel_id=1, source_target_pairs={{0,1},{1,2},{2,3},{3,4},{4,5},{5,6},{6,7},{7,8},{8,9},{9,10},{10,1... | collective-permute-start | bytes 294920 | tf_op jit(solution)/shard_map/ppermute | solution.py:29
  497.8 18.4 %collective-permute-start.69 = (f32[32,768]{1,0:T(8,128)S(1)}, f32[32,768]{1,0:T(8,128)S(1)}, u32[]{:S(2)}, u32[]{:S(2)}) collective-permute-start(f32[32,768]{1,0:T(8,128)S(1)} %reshape.1069), channel_id=1, source_target_pairs={{0,15},{1,0},{2,1},{3,2},{4,3},{5,4},{6,5},{7,6},{8,7},{9,8},{10,9... | collective-permute-start | bytes 294920 | tf_op jit(solution)/shard_map/ppermute | solution.py:34
  547.3 9.0 collective-permute-start.78
  548.0 9.0 collective-permute-start.79
  556.9 8.5 collective-permute-start.81
  589.4 33.2 %collective-permute-start.85 = (f32[32,768]{1,0:T(8,128)}, f32[32,768]{1,0:T(8,128)}, u32[]{:S(2)}, u32[]{:S(2)}) collective-permute-start(f32[32,768]{1,0:T(8,128)} %reshape.1088), channel_id=1, source_target_pairs={{0,1},{1,2},{2,3},{3,4},{4,5},{5,6},{6,7},{7,8},{8,9},{9,10},{10,1... | collective-permute-start | bytes 294920 | tf_op jit(solution)/shard_map/ppermute | solution.py:29
  589.4 34.8 %collective-permute-start.86 = (f32[32,768]{1,0:T(8,128)}, f32[32,768]{1,0:T(8,128)}, u32[]{:S(2)}, u32[]{:S(2)}) collective-permute-start(f32[32,768]{1,0:T(8,128)} %reshape.1088), channel_id=1, source_target_pairs={{0,15},{1,0},{2,1},{3,2},{4,3},{5,4},{6,5},{7,6},{8,7},{9,8},{10,9... | collective-permute-start | bytes 294920 | tf_op jit(solution)/shard_map/ppermute | solution.py:34
  602.0 10.8 %collective-permute-start.101 = (f32[3,8,256]{2,1,0:T(8,128)}, f32[3,8,256]{2,1,0:T(8,128)}, u32[]{:S(2)}, u32[]{:S(2)}) collective-permute-start(f32[3,8,256]{2,1,0:T(8,128)} %bitcast.758), channel_id=1, source_target_pairs={{16,0},{32,16},{48,32},{64,48},{80,64},{96,80},{112,96},{17,1},{33... | collective-permute-start | bytes 73736 | tf_op jit(solution)/shard_map/ppermute | solution.py:47
  622.6 8.5 collective-permute-start.87
  647.9 8.3 collective-permute-start.94
  656.2 8.6 collective-permute-start.96
  662.9 9.0 collective-permute-start.97
  711.9 34.2 %collective-permute-start.102 = (f32[32,768]{1,0:T(8,128)}, f32[32,768]{1,0:T(8,128)}, u32[]{:S(2)}, u32[]{:S(2)}) collective-permute-start(f32[32,768]{1,0:T(8,128)} %reshape.1107), channel_id=1, source_target_pairs={{0,1},{1,2},{2,3},{3,4},{4,5},{5,6},{6,7},{7,8},{8,9},{9,10},{10,1... | collective-permute-start | bytes 294920 | tf_op jit(solution)/shard_map/ppermute | solution.py:29
  712.0 35.8 %collective-permute-start.103 = (f32[32,768]{1,0:T(8,128)}, f32[32,768]{1,0:T(8,128)}, u32[]{:S(2)}, u32[]{:S(2)}) collective-permute-start(f32[32,768]{1,0:T(8,128)} %reshape.1107), channel_id=1, source_target_pairs={{0,15},{1,0},{2,1},{3,2},{4,3},{5,4},{6,5},{7,6},{8,7},{9,8},{10,9... | collective-permute-start | bytes 294920 | tf_op jit(solution)/shard_map/ppermute | solution.py:34
  720.2 8.9 collective-permute-start.117
  725.5 10.8 %collective-permute-start.118 = (f32[3,8,256]{2,1,0:T(8,128)}, f32[3,8,256]{2,1,0:T(8,128)}, u32[]{:S(2)}, u32[]{:S(2)}) collective-permute-start(f32[3,8,256]{2,1,0:T(8,128)} %bitcast.756), channel_id=1, source_target_pairs={{16,0},{32,16},{48,32},{64,48},{80,64},{96,80},{112,96},{17,1},{33... | collective-permute-start | bytes 73736 | tf_op jit(solution)/shard_map/ppermute | solution.py:47
  746.2 8.5 collective-permute-start.104
  779.4 8.4 collective-permute-start.113
  786.6 9.0 collective-permute-start.114
  787.8 8.5 collective-permute-start.115
  832.7 19.9 %collective-permute-start.119 = (f32[32,768]{1,0:T(8,128)}, f32[32,768]{1,0:T(8,128)}, u32[]{:S(2)}, u32[]{:S(2)}) collective-permute-start(f32[32,768]{1,0:T(8,128)} %reshape.1127), channel_id=1, source_target_pairs={{0,1},{1,2},{2,3},{3,4},{4,5},{5,6},{6,7},{7,8},{8,9},{9,10},{10,1... | collective-permute-start | bytes 294920 | tf_op jit(solution)/shard_map/ppermute | solution.py:29
  832.7 21.5 %collective-permute-start.120 = (f32[32,768]{1,0:T(8,128)}, f32[32,768]{1,0:T(8,128)}, u32[]{:S(2)}, u32[]{:S(2)}) collective-permute-start(f32[32,768]{1,0:T(8,128)} %reshape.1127), channel_id=1, source_target_pairs={{0,15},{1,0},{2,1},{3,2},{4,3},{5,4},{6,5},{7,6},{8,7},{9,8},{10,9... | collective-permute-start | bytes 294920 | tf_op jit(solution)/shard_map/ppermute | solution.py:34
  852.6 8.5 collective-permute-start.121
  885.8 8.6 collective-permute-start.130
  892.9 8.9 collective-permute-start.131
  (231 other events, 1798.7 us)
